TPU v7x, 32 devices: a whole 2x2x4 slice. The times are simulated.
32 devices in a mesh: space: 2 (over core), energy: 8 (over z, y), mom: 2 (over x).
Axes of the slice: x: 2, y: 2, z: 4, core: 2. Of those that a mesh axis runs over, the one named last changes fastest.
Arguments:
- hamiltonian: float32 [2, 256, 256], P('space'), may hold values from -0.375 to 0.375
- coupling: float32 [2, 224, 224], P('space'), may hold values from -0.75 to 0.75
- self_energy: float32 [2, 8, 4, 2, 256, 256], P('space', 'energy', 'mom'), may hold values from -0.375 to 0.375
- pattern: int32 [2, 256, 256], P('space', 'energy'), may hold values 0 or 1
- momentum_table: int32 [4, 4], replicated, may hold values from 0 to 3
- momentum_weights: float32 [4], replicated, may hold values from 0.2 to 1
- mode_strengths: float32 [2], replicated, may hold values from 0.3 to 1
- mode_offsets: int32 [2], replicated, may hold values from 1 to 5
Outputs:
- new_self_energy: float32 [2, 8, 4, 2, 256, 256], P('space', 'energy', 'mom')
Inputs may be any that keep to these rules, and one draw needn't show every extreme that they name: `momentum_table`: entry [k, q] is the momentum index whose Green's function reaches momentum k through transfer q.
All inputs are finite; a program needn't handle non-finite values. No bound on the sum of `pattern` on one device may be relied on, other than what follows from the above.
Results may differ from a plain program's by a relative error of at most 0.0001.
Values sent between devices are 32-bit elements; how exact they have to be, the bound alone decides.
No kernel may reach another device: no remote copies, remote signals or barrier semaphores. Data moves between devices by JAX's collectives and lax.ppermute only.
A program may use at most 128 MiB of HBM per device.

v0:
```python
import jax
import jax.numpy as jnp
from jax import lax
from jax.sharding import PartitionSpec as P

broadening = 1.0
contact = 1.0
dispersion = 1.0


def from_behind(shard, axis, by):
    count = lax.axis_size(axis)
    pairs = [(i, i + by) for i in range(count) if 0 <= i + by < count]
    return lax.ppermute(shard, axis, pairs)


def matmul_highest(left_side, right_side):
    return jnp.einsum("...ij,...jk->...ik", left_side, right_side, precision=lax.Precision.HIGHEST)


def product_complex(left_side, right_side):
    left_real = left_side[..., 0, :, :]
    left_imag = left_side[..., 1, :, :]
    right_real = right_side[..., 0, :, :]
    right_imag = right_side[..., 1, :, :]
    real_part = matmul_highest(left_real, right_real) - matmul_highest(left_imag, right_imag)
    imag_part = matmul_highest(left_real, right_imag) + matmul_highest(left_imag, right_real)
    return jnp.stack([real_part, imag_part], axis=-3)


def approximate_inverse(matrix):
    order_size = matrix.shape[-1]
    identity = jnp.eye(order_size, dtype=jnp.float32)
    real_part = matrix[..., 0, :, :]
    imag_part = matrix[..., 1, :, :]
    diag_real = jnp.diagonal(real_part, axis1=-2, axis2=-1)
    diag_imag = jnp.diagonal(imag_part, axis1=-2, axis2=-1)
    modulus = diag_real * diag_real + diag_imag * diag_imag
    inverse_real = diag_real / modulus
    inverse_imag = -diag_imag / modulus
    outside = 1.0 - identity
    off_real = real_part * outside
    off_imag = imag_part * outside
    row_real = inverse_real[..., :, None]
    row_imag = inverse_imag[..., :, None]
    scaled = jnp.stack(
        [row_real * off_real - row_imag * off_imag, row_real * off_imag + row_imag * off_real],
        axis=-3,
    )
    series = product_complex(scaled, scaled) - scaled
    series_real = series[..., 0, :, :] + identity
    series_imag = series[..., 1, :, :]
    column_real = inverse_real[..., None, :]
    column_imag = inverse_imag[..., None, :]
    return jnp.stack(
        [
            series_real * column_real - series_imag * column_imag,
            series_real * column_imag + series_imag * column_real,
        ],
        axis=-3,
    )


def build_system(
    hamiltonian_slice, self_slice, energy_index, momentum_index, energies_all, momenta_all
):
    order_size = hamiltonian_slice.shape[-1]
    identity = jnp.eye(order_size, dtype=jnp.float32)
    symmetric = 0.5 * (hamiltonian_slice + hamiltonian_slice.T)
    energy = -2.0 + 4.0 * energy_index.astype(jnp.float32) / energies_all
    kinetic = dispersion * (
        1.0 - jnp.cos(2.0 * jnp.pi * momentum_index.astype(jnp.float32) / momenta_all)
    )
    diagonal_shift = energy[:, None] - kinetic[None, :]
    real_part = diagonal_shift[:, :, None, None] * identity - symmetric - self_slice[:, :, 0]
    imag_part = broadening * identity - self_slice[:, :, 1]
    return jnp.stack([real_part, imag_part], axis=2)


def contact_term(surface):
    return jnp.stack(
        [jnp.zeros((surface, surface), jnp.float32), -contact * jnp.eye(surface, dtype=jnp.float32)]
    )


def embed_first(matrix, term):
    width = term.shape[-1]
    return matrix.at[..., :width, :width].add(-term)


def embed_last(matrix, term):
    width = term.shape[-1]
    order_size = matrix.shape[-1]
    return matrix.at[..., order_size - width :, order_size - width :].add(-term)


def sandwich(coupling_block, middle):
    return jnp.einsum(
        "ji,...jk,kl->...il",
        coupling_block,
        middle,
        coupling_block,
        precision=lax.Precision.HIGHEST,
    )


def sandwich_back(coupling_block, middle):
    return jnp.einsum(
        "ij,...jk,lk->...il",
        coupling_block,
        middle,
        coupling_block,
        precision=lax.Precision.HIGHEST,
    )


def convolve_energy(green_rows, mode_strengths, mode_offsets):
    point_count = green_rows.shape[0]
    widths = [(point_count, point_count)] + [(0, 0)] * (green_rows.ndim - 1)
    padded = jnp.pad(green_rows, widths)
    accumulated = jnp.zeros_like(green_rows)
    for mode_index in range(mode_strengths.shape[0]):
        offset_now = mode_offsets[mode_index]
        below_part = lax.dynamic_slice_in_dim(padded, point_count - offset_now, point_count, 0)
        above_part = lax.dynamic_slice_in_dim(padded, point_count + offset_now, point_count, 0)
        accumulated = accumulated + mode_strengths[mode_index] * (below_part + above_part)
    return accumulated


def momentum_coefficients(momentum_table, momentum_weights):
    momentum_count = momentum_table.shape[0]
    labels = jnp.arange(momentum_count, dtype=jnp.int32)
    matches = (momentum_table[:, :, None] == labels[None, None, :]).astype(jnp.float32)
    return jnp.einsum("q,kqj->kj", momentum_weights, matches, precision=lax.Precision.HIGHEST)


def keep_state(held_terms, message):
    return (held_terms, message)


def body(
    hamiltonian,
    coupling,
    self_energy,
    pattern,
    momentum_table,
    momentum_weights,
    mode_strengths,
    mode_offsets,
):
    orbitals = hamiltonian.shape[-1]
    surface = coupling.shape[-1]
    energies_here = self_energy.shape[1]
    momenta_here = self_energy.shape[2]
    energy_groups = lax.axis_size("energy")
    momentum_groups = lax.axis_size("mom")
    slices = lax.axis_size("space")
    position = lax.axis_index("space")
    energies_all = energies_here * energy_groups
    momenta_all = momenta_here * momentum_groups
    energy_index = lax.axis_index("energy") * energies_here + jnp.arange(
        energies_here, dtype=jnp.int32
    )
    momentum_index = lax.axis_index("mom") * momenta_here + jnp.arange(
        momenta_here, dtype=jnp.int32
    )
    item_count = energies_here * momenta_here
    system = build_system(
        hamiltonian[0], self_energy[0], energy_index, momentum_index, energies_all, momenta_all
    )
    system = system.reshape(item_count, 2, orbitals, orbitals)
    coupling_block = coupling[0]
    corner = orbitals - surface
    first_slice = position == 0
    last_slice = position == slices - 1
    zero_terms = jnp.zeros((item_count, 2, surface, surface), jnp.float32)
    single_source = contact_term(surface)
    zero_message = jnp.zeros((2, surface, surface), jnp.float32)

    def forward_turn(sweep_step, carry):
        received = from_behind(carry[1], "space", 1)
        item_now = sweep_step - position

        def forward_active(held_terms, message):
            incoming = jnp.where(first_slice, single_source, received)
            current = lax.dynamic_index_in_dim(system, item_now, 0, keepdims=False)
            green_left = approximate_inverse(embed_first(current, incoming))
            stored = lax.dynamic_update_index_in_dim(held_terms, incoming, item_now, 0)
            return (stored, sandwich(coupling_block, green_left[..., corner:, corner:]))

        return lax.cond(
            (item_now >= 0) & (item_now < item_count),
            forward_active,
            keep_state,
            carry[0],
            carry[1],
        )

    def backward_turn(sweep_step, carry):
        received = from_behind(carry[1], "space", -1)
        item_now = sweep_step - (slices - 1 - position)

        def backward_active(held_terms, message):
            incoming = jnp.where(last_slice, single_source, received)
            right_now = sandwich_back(coupling_block, incoming)
            current = lax.dynamic_index_in_dim(system, item_now, 0, keepdims=False)
            green_right = approximate_inverse(embed_last(current, right_now))
            stored = lax.dynamic_update_index_in_dim(held_terms, right_now, item_now, 0)
            return (stored, green_right[..., :surface, :surface])

        return lax.cond(
            (item_now >= 0) & (item_now < item_count),
            backward_active,
            keep_state,
            carry[0],
            carry[1],
        )

    turn_total = slices + item_count - 1
    left_terms, unused_left = lax.fori_loop(0, turn_total, forward_turn, (zero_terms, zero_message))
    right_terms, unused_right = lax.fori_loop(
        0, turn_total, backward_turn, (zero_terms, zero_message)
    )
    green_final = approximate_inverse(embed_last(embed_first(system, left_terms), right_terms))
    coefficients = momentum_coefficients(momentum_table, momentum_weights)
    mask_rows = pattern[0].astype(jnp.float32)
    row_count = orbitals // energy_groups
    blocks = green_final.reshape(energies_here, momenta_here, 2, energy_groups, row_count, orbitals)
    regrouped = lax.all_to_all(blocks, "energy", split_axis=3, concat_axis=0, tiled=True)
    regrouped = regrouped.reshape(energies_all, momenta_here, 2, row_count, orbitals)
    phonon = convolve_energy(regrouped, mode_strengths, mode_offsets)
    own_rows = lax.dynamic_slice_in_dim(
        coefficients, lax.axis_index("mom") * momenta_here, momenta_here, 0
    )
    mixed_terms = jnp.zeros_like(phonon) + jnp.einsum(
        "kj,ej...->ek...",
        own_rows,
        lax.all_gather(phonon, "mom", axis=1, tiled=True),
        precision=lax.Precision.HIGHEST,
    )
    mixed_terms = mixed_terms * mask_rows
    mixed_terms = mixed_terms.reshape(energies_all, momenta_here, 2, 1, row_count, orbitals)
    returned = lax.all_to_all(mixed_terms, "energy", split_axis=0, concat_axis=3, tiled=True)
    return returned.reshape(1, energies_here, momenta_here, 2, orbitals, orbitals)


def solution(mesh):
    return jax.shard_map(
        body,
        mesh=mesh,
        in_specs=(
            P("space", None, None),
            P("space", None, None),
            P("space", "energy", "mom", None, None, None),
            P("space", "energy", None),
            P(),
            P(),
            P(),
            P(),
        ),
        out_specs=P("space", "energy", "mom", None, None, None),
        check_vma=False,
    )
```

profile of v0, /device:TPU:0, one launch (start us, length us, event | category | flops | bytes accessed | tf_op | source)
XLA Modules:
  0.0 275.0 jit_solution(17039815926781231370)
XLA Ops:
  15.1 32.7 %while.36 = (s32[]{:T(128)}, f32[2,2,224,224]{3,2,1,0:T(8,128)}, f32[2,224,224]{2,1,0:T(8,128)S(1)}, s32[]{:T(128)}, pred[]{:T(512)}, /*index=5*/f32[2,224,224]{...) while((s32[]{:T(128)}, f32[2,2,224,224]{3,2,1,0:T(8,128)}, ...), condition=%wide.region_3.0_spmd, body=%wide.region_0.3_spmd.sunk | while | flops 1347138048 | bytes 16336718 | solution.py:220
  15.1 2.4 collective-permute-start
  19.0 11.2 %conditional.4 = ((f32[2,2,224,224]{3,2,1,0:T(8,128)}, f32[2,224,224]{2,1,0:T(8,128)S(1)})) conditional(s32[]{:T(128)} %convert_element_type.173, (f32[2,2,224,224]{3,2,1,0:T(8,128)}, f32[2,224,224]{2,1,0:T(8,128)S(1)}) %tuple.116, (pred[]{:T(512)}, f32[2,224,224]{2,1,0:T(8,128)S(1)}, f32[2,224,224]{2,1,0:T(8,128)S(1)}, s32[]{:T(128)}, ...), branch_computations={%region_1.0_spmd, %region_2.2_spmd} | conditional | flops 1347138048 | bytes 14730827 | solution.py:191
  21.5 2.3 gather_fusion
  23.8 2.3 gather_fusion.1
  32.9 11.3 %conditional.4 = ((f32[2,2,224,224]{3,2,1,0:T(8,128)}, f32[2,224,224]{2,1,0:T(8,128)S(1)})) conditional(s32[]{:T(128)} %convert_element_type.173, (f32[2,2,224,224]{3,2,1,0:T(8,128)}, f32[2,224,224]{2,1,0:T(8,128)S(1)}) %tuple.116, (pred[]{:T(512)}, f32[2,224,224]{2,1,0:T(8,128)S(1)}, f32[2,224,224]{2,1,0:T(8,128)S(1)}, s32[]{:T(128)}, ...), branch_computations={%region_1.0_spmd, %region_2.2_spmd} | conditional | flops 1347138048 | bytes 14730827 | solution.py:191
  35.4 2.3 gather_fusion
  37.8 2.3 gather_fusion.1
  49.4 5.2 %scatter-add.16 = f32[2,2,256,256]{3,2,0,1:T(8,128)} dynamic-update-slice(f32[2,2,256,256]{3,2,0,1:T(8,128)} %copy-done.2, f32[2,2,224,224]{3,2,0,1:T(8,128)S(1)} %fusion.55, s32[]{:T(128)} %constant.266.clone.1, s32[]{:T(128)} %constant.266.clone.1, s32[]{:T(128)} %constant.266.clone.1, s32[]{:T(128)} %constant.266.clone.1) | dynamic-update-slice | bytes 1605636 | tf_op jit(solution)/shard_map/scatter-add | solution.py:88
  55.7 61.7 %while.37 = (s32[]{:T(128)}, f32[2,2,224,224]{3,2,1,0:T(8,128)}, f32[2,224,224]{2,1,0:T(8,128)S(1)}, s32[]{:T(128)}, pred[]{:T(512)}, /*index=5*/f32[2,224,224]{...) while((s32[]{:T(128)}, f32[2,2,224,224]{3,2,1,0:T(8,128)}, ...), condition=%wide.region_7.8_spmd, body=%wide.region_4.7_spmd.sunk | while | flops 1347037696 | bytes 17139036 | solution.py:221
  57.4 13.1 %collective-permute-done.1 = f32[2,224,224]{1,2,0:T(8,128)} collective-permute-done((f32[2,224,224]{1,2,0:T(8,128)S(1)}, f32[2,224,224]{1,2,0:T(8,128)}, u32[]{:S(2)}, u32[]{:S(2)}) %collective-permute-start.1) | collective-permute-done | bytes 401440 | tf_op jit(solution)/shard_map/while/body/eval_jaxpr/ppermute | solution.py:14
  72.0 14.8 %collective-permute-done.1 = f32[2,224,224]{1,2,0:T(8,128)} collective-permute-done((f32[2,224,224]{1,2,0:T(8,128)S(1)}, f32[2,224,224]{1,2,0:T(8,128)}, u32[]{:S(2)}, u32[]{:S(2)}) %collective-permute-start.1) | collective-permute-done | bytes 401440 | tf_op jit(solution)/shard_map/while/body/eval_jaxpr/ppermute | solution.py:14
  86.8 13.3 %conditional.5 = ((f32[2,2,224,224]{3,2,1,0:T(8,128)}, f32[2,224,224]{2,1,0:T(8,128)S(1)})) conditional(s32[]{:T(128)} %convert_element_type.174, (f32[2,2,224,224]{3,2,1,0:T(8,128)}, f32[2,224,224]{2,1,0:T(8,128)S(1)}) %tuple.119, (pred[]{:T(512)}, f32[2,224,224]{1,2,0:T(8,128)}, f32[2,224,224]{1,2,0:T(8,128)}, f32[224,224]{1,0:T(8,128)S(1)}, ...), branch_computations={%region_5.5_spmd, %region_6.6_spmd} | conditional | flops 1347037696 | bytes 14730331 | solution.py:211
  90.0 3.4 %scatter-add.10 = f32[2,256,256]{2,1,0:T(8,128)S(1)} dynamic-update-slice(f32[2,256,256]{2,1,0:T(8,128)S(1)} %dynamic-slice_bitcast_fusion.2, f32[2,224,224]{2,1,0:T(8,128)S(1)} %fusion.22, s32[]{:T(128)} %constant.251.clone, s32[]{:T(128)} %constant.253.clone, s32[]{:T(128)} %constant.253.clone) | dynamic-update-slice | bytes 802820 | tf_op jit(solution)/shard_map/while/body/eval_jaxpr/cond/branch_1_fun/scatter-add | solution.py:94
  93.4 2.3 gather_fusion.2
  95.8 2.3 gather_fusion.3
  101.6 2.5 collective-permute-done.1
  104.1 13.3 %conditional.5 = ((f32[2,2,224,224]{3,2,1,0:T(8,128)}, f32[2,224,224]{2,1,0:T(8,128)S(1)})) conditional(s32[]{:T(128)} %convert_element_type.174, (f32[2,2,224,224]{3,2,1,0:T(8,128)}, f32[2,224,224]{2,1,0:T(8,128)S(1)}) %tuple.119, (pred[]{:T(512)}, f32[2,224,224]{1,2,0:T(8,128)}, f32[2,224,224]{1,2,0:T(8,128)}, f32[224,224]{1,0:T(8,128)S(1)}, ...), branch_computations={%region_5.5_spmd, %region_6.6_spmd} | conditional | flops 1347037696 | bytes 14730331 | solution.py:211
  107.3 3.4 %scatter-add.10 = f32[2,256,256]{2,1,0:T(8,128)S(1)} dynamic-update-slice(f32[2,256,256]{2,1,0:T(8,128)S(1)} %dynamic-slice_bitcast_fusion.2, f32[2,224,224]{2,1,0:T(8,128)S(1)} %fusion.22, s32[]{:T(128)} %constant.251.clone, s32[]{:T(128)} %constant.253.clone, s32[]{:T(128)} %constant.253.clone) | dynamic-update-slice | bytes 802820 | tf_op jit(solution)/shard_map/while/body/eval_jaxpr/cond/branch_1_fun/scatter-add | solution.py:94
  110.8 2.3 gather_fusion.2
  113.2 2.3 gather_fusion.3
  118.9 7.0 %scatter-add.17 = f32[2,2,256,256]{3,2,0,1:T(8,128)S(1)} dynamic-update-slice(f32[2,2,256,256]{3,2,0,1:T(8,128)S(1)} %copy-done.3, f32[2,2,224,224]{3,2,0,1:T(8,128)S(1)} %slice_add_fusion, s32[]{:T(128)} %constant.266.clone.1, s32[]{:T(128)} %constant.266.clone.1, s32[]{:T(128)} %constant.271.clone.1, s32[]{:T(128)} %constant.271.clone.1) | dynamic-update-slice | bytes 1605636 | tf_op jit(solution)/shard_map/scatter-add | solution.py:94
  126.1 16.5 %copy.78 = f32[2,256,256]{0,2,1:T(8,128)} copy(f32[2,256,256]{2,1,0:T(8,128)S(1)} %get-tuple-element.573) | data formatting | bytes 1048576 | tf_op jit(solution)/shard_map/squeeze | solution.py:34
  142.5 2.3 gather_fusion.4
  145.0 16.4 %copy.80 = f32[2,256,256]{0,2,1:T(8,128)} copy(f32[2,256,256]{2,1,0:T(8,128)S(1)} %get-tuple-element.574) | data formatting | bytes 1048576 | tf_op jit(solution)/shard_map/squeeze | solution.py:35
  161.4 2.3 gather_fusion.5
  169.8 6.6 %all-to-all-start = ((f32[1,2,2,8,32,256]{5,1,4,2,0,3:T(2,128)}), f32[1,2,2,8,32,256]{5,1,4,2,0,3:T(2,128)S(1)}, u32[]{:S(2)}, u32[]{:S(2)}) async-start(f32[1,2,2,8,32,256]{5,1,4,2,0,3:T(2,128)} %pad_maximum_fusion.4), calls=%async_computation | async-start | bytes 2097152 | tf_op jit(solution)/shard_map/all_to_all | solution.py:229
  182.6 10.2 %all-to-all-done = f32[1,2,2,8,32,256]{5,1,4,2,0,3:T(2,128)S(1)} async-done(((f32[1,2,2,8,32,256]{5,1,4,2,0,3:T(2,128)}), f32[1,2,2,8,32,256]{5,1,4,2,0,3:T(2,128)S(1)}, u32[]{:S(2)}, u32[]{:S(2)}) %all-to-all-start) | async-done | bytes 1048608 | tf_op jit(solution)/shard_map/all_to_all | solution.py:229
  192.8 3.7 %multiply_add_fusion.6 = f32[8,2,2,32,256]{4,1,3,2,0:T(2,128)S(1)} fusion(s32[]{:T(128)S(6)} %select_n.58, f32[8,2,2,32,256]{4,1,3,2,0:T(2,128)S(1)} %bitcast.181, s32[]{:T(128)S(6)} %select_n.57, s32[]{:T(128)S(6)} %select_n.56, s32[]{:T(128)S(6)} %select_n.55, f32[]{:T(128)} %bitcast.46, f32[]{:T(128)} %bitcast.22), kind=kLoop, calls=%fused_computation.106 | loop fusion | flops 1310720 | bytes 2097176 | tf_op jit(solution)/shard_map/add | solution.py:126
  197.9 31.6 %all-gather.2.cloned.1.call-done = f32[8,4,2,32,256]{4,3,2,0,1:T(8,128)} async-done(((f32[8,2,2,32,256]{4,3,2,0,1:T(8,128)}), f32[8,4,2,32,256]{4,3,2,0,1:T(8,128)}) %all-gather.2.cloned.1.call-update) | async-done | bytes 2097168 | tf_op jit(solution)/shard_map/all_gather | solution.py:238
  229.5 6.5 %fusion.45 = f32[8,2,2,1,32,256]{5,1,4,2,3,0:T(2,128)S(1)} fusion(f32[8,4,2,32,256]{4,3,2,0,1:T(8,128)} %all-gather.2.cloned.1.call-done, f32[32,256]{1,0:T(8,128)S(1)} %convert_bitcast_fusion, f32[4,4]{1,0:T(4,128)S(1)} %bitcast.186, s32[]{:T(128)S(6)} %select_n.59), kind=kOutput, calls=%fused_computation.92 | convolution fusion | flops 12845056 | bytes 3179524 | tf_op jit(solution)/shard_map/kj,ej...->ek.../dot_general | solution.py:235
  236.1 30.9 %all_to_all.30 = f32[8,2,2,1,32,256]{5,1,4,2,3,0:T(2,128)S(1)} all-to-all(f32[8,2,2,1,32,256]{5,1,4,2,3,0:T(2,128)S(1)} %fusion.45), channel_id=1, replica_groups=mesh['space'=2,'energy'=8,'mom'=2] {'energy'}, dimensions={0} | all-to-all | bytes 2097152 | tf_op jit(solution)/shard_map/all_to_all | solution.py:243
  (145 shorter events, 57.8 us)
Async XLA Ops:
  6.5 191.1 %copy-start = (f32[4]{0:T(128)S(1)}, f32[4]{0:T(128)}, u32[]{:S(2)}) copy-start(f32[4]{0:T(128)} %param.29) | copy-start | bytes 52
  6.5 3.2 %copy-start.9 = (f32[1,256,256]{2,1,0:T(8,128)S(1)}, f32[1,256,256]{2,1,0:T(8,128)}, u32[]{:S(2)}) copy-start(f32[1,256,256]{2,1,0:T(8,128)} %param.24) | copy-start | bytes 786436
  6.6 3.4 %copy-start.7 = (f32[256,256]{1,0:T(8,128)}, f32[256,256]{1,0:T(8,128)S(1)}, u32[]{:S(2)}) copy-start(f32[256,256]{1,0:T(8,128)S(1)} %fusion.57) | copy-start | bytes 786436
  10.0 0.8 copy-start.4
  10.0 1.0 copy-start.5
  11.0 4.1 %copy-start.1 = (f32[1,224,224]{2,1,0:T(8,128)S(1)}, f32[1,224,224]{2,1,0:T(8,128)}, u32[]{:S(2)}) copy-start(f32[1,224,224]{2,1,0:T(8,128)} %param.25) | copy-start | bytes 602116
  11.1 1.0 copy-start.2
  15.1 3.8 %collective-permute-start = (f32[2,224,224]{2,1,0:T(8,128)S(1)}, f32[2,224,224]{2,1,0:T(8,128)S(1)}, u32[]{:S(2)}, u32[]{:S(2)}) collective-permute-start(f32[2,224,224]{2,1,0:T(8,128)S(1)} %get-tuple-element.708), channel_id=1, source_target_pairs={{0,16},{1,17},{2,18},{3,19},{4,20},{5,21},{6,22},{7,23},{8,24},{9,... | collective-permute-start | bytes 1204232 | tf_op jit(solution)/shard_map/while/body/eval_jaxpr/ppermute | solution.py:14
  30.2 2.7 collective-permute-start
  44.2 3.7 %collective-permute-start = (f32[2,224,224]{2,1,0:T(8,128)S(1)}, f32[2,224,224]{2,1,0:T(8,128)S(1)}, u32[]{:S(2)}, u32[]{:S(2)}) collective-permute-start(f32[2,224,224]{2,1,0:T(8,128)S(1)} %get-tuple-element.708), channel_id=1, source_target_pairs={{0,16},{1,17},{2,18},{3,19},{4,20},{5,21},{6,22},{7,23},{8,24},{9,... | collective-permute-start | bytes 1204232 | tf_op jit(solution)/shard_map/while/body/eval_jaxpr/ppermute | solution.py:14
  55.7 61.7 %copy-start.3 = (f32[2,2,256,256]{3,2,0,1:T(8,128)S(1)}, f32[2,2,256,256]{3,2,0,1:T(8,128)}, u32[]{:S(2)}) copy-start(f32[2,2,256,256]{3,2,0,1:T(8,128)} %scatter-add.16) | copy-start | bytes 3145732
  55.9 14.5 %collective-permute-start.1 = (f32[2,224,224]{1,2,0:T(8,128)S(1)}, f32[2,224,224]{1,2,0:T(8,128)}, u32[]{:S(2)}, u32[]{:S(2)}) collective-permute-start(f32[2,224,224]{1,2,0:T(8,128)S(1)} %copy.110), channel_id=1, source_target_pairs={{16,0},{17,1},{18,2},{19,3},{20,4},{21,5},{22,6},{23,7},{24,8},{25... | collective-permute-start | bytes 1204232 | tf_op jit(solution)/shard_map/while/body/eval_jaxpr/ppermute | solution.py:14
  70.6 16.1 %collective-permute-start.1 = (f32[2,224,224]{1,2,0:T(8,128)S(1)}, f32[2,224,224]{1,2,0:T(8,128)}, u32[]{:S(2)}, u32[]{:S(2)}) collective-permute-start(f32[2,224,224]{1,2,0:T(8,128)S(1)} %copy.110), channel_id=1, source_target_pairs={{16,0},{17,1},{18,2},{19,3},{20,4},{21,5},{22,6},{23,7},{24,8},{25... | collective-permute-start | bytes 1204232 | tf_op jit(solution)/shard_map/while/body/eval_jaxpr/ppermute | solution.py:14
  100.3 3.8 %collective-permute-start.1 = (f32[2,224,224]{1,2,0:T(8,128)S(1)}, f32[2,224,224]{1,2,0:T(8,128)}, u32[]{:S(2)}, u32[]{:S(2)}) collective-permute-start(f32[2,224,224]{1,2,0:T(8,128)S(1)} %copy.110), channel_id=1, source_target_pairs={{16,0},{17,1},{18,2},{19,3},{20,4},{21,5},{22,6},{23,7},{24,8},{25... | collective-permute-start | bytes 1204232 | tf_op jit(solution)/shard_map/while/body/eval_jaxpr/ppermute | solution.py:14
  144.9 18.9 %copy-start.6 = (f32[256,256]{1,0:T(8,128)S(1)}, f32[256,256]{1,0:T(8,128)}, u32[]{:S(2)}) copy-start(f32[256,256]{1,0:T(8,128)} %broadcast_subtract_fusion) | copy-start | bytes 786436
  166.3 1.0 copy-start.8
  167.4 9.3 %copy-start.11 = (s32[2]{0:T(128)S(1)}, s32[2]{0:T(128)}, u32[]{:S(2)}) copy-start(s32[2]{0:T(128)} %param.31) | copy-start | bytes 28
  167.4 14.6 %copy-start.12 = (f32[2]{0:T(128)S(1)}, f32[2]{0:T(128)}, u32[]{:S(2)}) copy-start(f32[2]{0:T(128)} %param.30) | copy-start | bytes 28
  169.8 23.0 %all-to-all-start = ((f32[1,2,2,8,32,256]{5,1,4,2,0,3:T(2,128)}), f32[1,2,2,8,32,256]{5,1,4,2,0,3:T(2,128)S(1)}, u32[]{:S(2)}, u32[]{:S(2)}) async-start(f32[1,2,2,8,32,256]{5,1,4,2,0,3:T(2,128)} %pad_maximum_fusion.4), calls=%async_computation | async-start | bytes 2097152 | tf_op jit(solution)/shard_map/all_to_all | solution.py:229
  176.4 21.3 %copy-start.13 = (s32[4,4]{1,0:T(4,128)S(1)}, s32[4,4]{1,0:T(4,128)}, u32[]{:S(2)}) copy-start(s32[4,4]{1,0:T(4,128)} %param.28) | copy-start | bytes 196
  176.4 21.5 %copy-start.10 = (s32[1,32,256]{2,1,0:T(8,128)S(1)}, s32[1,32,256]{2,1,0:T(8,128)}, u32[]{:S(2)}) copy-start(s32[1,32,256]{2,1,0:T(8,128)} %param.27) | copy-start | bytes 98308
  176.4 53.1 %all-gather.2.cloned.1.call-start = ((), (), s32[]{:S(2)}) async-start(), calls=%async_computation.2 | async-start | bytes 3145728 | tf_op jit(solution)/shard_map/all_gather | solution.py:238
Sparse Core Ops, SparseCore 0:
  197.8 31.6 all-gather.1
where the time goes:
time: 276 us; the launch traced here: 275 us
  local copies, waits for them, and re-layouts  93.8 us (34%)
  waiting for transfers between devices  76.4 us (28%)
  blocking collectives  30.9 us (11%)
  matrix products  24 us (9%)
  between operations  18.5 us (7%)
  starting transfers between devices  16.9 us (6%)
  other arithmetic  13.6 us (5%)
    ppermute x6, waiting for transfers between devices, from_behind(): return lax.ppermute(shard, axis, pairs)  34.6 us
    all_gather x1, waiting for transfers between devices, body(): lax.all_gather(phonon, 'mom', axis=1, tiled=True)  31.6 us
    all_to_all x1, blocking collectives, body(): lax.all_to_all(mixed_terms, 'energy', split_axis=0, concat_axis=3, tiled=...  30.9 us
    squeeze x6, local copies, waits for them, and re-layouts, approximate_inverse(): real_part = matrix[..., 0, :, :]  16.7 us
    squeeze x1, local copies, waits for them, and re-layouts, approximate_inverse(): imag_part = matrix[..., 1, :, :]  16.4 us
    scatter-add x3, local copies, waits for them, and re-layouts, embed_last(): return matrix.at[..., order_size - width:, order_size - width:].add(-term)  13.8 us
    gather x6, local copies, waits for them, and re-layouts, approximate_inverse(): diag_real = jnp.diagonal(real_part, axis1=-2, axis2=-1)  11.8 us
    gather x6, local copies, waits for them, and re-layouts, approximate_inverse(): diag_imag = jnp.diagonal(imag_part, axis1=-2, axis2=-1)  11.8 us
  transfers between devices with their start and end apart: 8, of which 8 were waited for; matrix products, arithmetic and copies ran while one was open for 0% of the time, Pallas kernels for 0%

commit v1 on v0

--- a/solution.py
+++ b/solution.py
@@ -6,6 +6,25 @@
 broadening = 1.0
 contact = 1.0
 dispersion = 1.0
+
+
+def attach_scales_on_mesh(values, dim_at):
+    part_next, high, opened = (lax.axis_size("mom"), lax.axis_index("mom"), values.shape[dim_at])
+    w1, u_next = (values, 1)
+    while u_next < part_next:
+        w1 = jnp.concatenate(
+            [
+                w1,
+                lax.ppermute(
+                    w1,
+                    axis_name="mom",
+                    perm=[(dev, (dev - u_next) % part_next) for dev in range(part_next)],
+                ),
+            ],
+            dim_at,
+        )
+        u_next = 2 * u_next
+    return jnp.roll(w1, high * opened, axis=dim_at)
 
 
 def from_behind(shard, axis, by):
@@ -235,7 +254,7 @@
     mixed_terms = jnp.zeros_like(phonon) + jnp.einsum(
         "kj,ej...->ek...",
         own_rows,
-        lax.all_gather(phonon, "mom", axis=1, tiled=True),
+        attach_scales_on_mesh(phonon, 1),
         precision=lax.Precision.HIGHEST,
     )
     mixed_terms = mixed_terms * mask_rows

time: 276 us -> 234 us (0.85)
  waiting for transfers between devices: 76.4 us -> 57.9 us
  between operations: 18.5 us -> 5.39 us
  blocking collectives: 30.9 us -> 18.9 us
    all_gather x1 -> x0, waiting for transfers between devices: 31.6 us -> none  [body(): lax.all_gather(phonon, 'mom', axis=1, tiled=True)]
    ppermute x0 -> x1, waiting for transfers between devices: none -> 13.1 us  [attach_scales_on_mesh(): lax.ppermute(w1, axis_name='mom', perm=[(dev, (dev - u_next) % part_next)...]
    all_to_all x1, blocking collectives: 30.9 us -> 18.9 us  [body(): lax.all_to_all(mixed_terms, 'energy', split_axis=0, concat_axis=3, tiled=...]
  transfers between devices with their start and end apart: 8 -> 8, of which waited for: 8 -> 8; matrix products, arithmetic and copies ran while one was open for 0% -> 1% of each run, Pallas kernels for 0% -> 0%
where the time goes in v1:
time: 234 us; the launch traced here: 233 us
  local copies, waits for them, and re-layouts  92.3 us (39%)
  waiting for transfers between devices  57.9 us (25%)
  matrix products  25.7 us (11%)
  blocking collectives  18.9 us (8%)
  starting transfers between devices  18.2 us (8%)
  other arithmetic  13.6 us (6%)
  between operations  5.39 us (2%)
    ppermute x6, waiting for transfers between devices, from_behind(): return lax.ppermute(shard, axis, pairs)  34.6 us
    all_to_all x1, blocking collectives, body(): lax.all_to_all(mixed_terms, 'energy', split_axis=0, concat_axis=3, tiled=...  18.9 us
    squeeze x6, local copies, waits for them, and re-layouts, approximate_inverse(): real_part = matrix[..., 0, :, :]  16.8 us
    squeeze x1, local copies, waits for them, and re-layouts, approximate_inverse(): imag_part = matrix[..., 1, :, :]  16.5 us
    scatter-add x3, local copies, waits for them, and re-layouts, embed_last(): return matrix.at[..., order_size - width:, order_size - width:].add(-term)  13.9 us
    ppermute x1, waiting for transfers between devices, attach_scales_on_mesh(): lax.ppermute(w1, axis_name='mom', perm=[(dev, (dev - u_next) % part_next)...  13.1 us
    gather x6, local copies, waits for them, and re-layouts, approximate_inverse(): diag_real = jnp.diagonal(real_part, axis1=-2, axis2=-1)  11.8 us
    gather x6, local copies, waits for them, and re-layouts, approximate_inverse(): diag_imag = jnp.diagonal(imag_part, axis1=-2, axis2=-1)  11.8 us
  transfers between devices with their start and end apart: 8, of which 8 were waited for; matrix products, arithmetic and copies ran while one was open for 1% of the time, Pallas kernels for 0%

profile of v1, /device:TPU:0, one launch (start us, length us, event | category | flops | bytes accessed | tf_op | source)
XLA Modules:
  0.0 232.8 jit_solution(16670871489499859884)
XLA Ops:
  7.9 32.8 %while.36 = (s32[]{:T(128)}, f32[2,2,224,224]{3,2,1,0:T(8,128)}, f32[2,224,224]{2,1,0:T(8,128)S(1)}, s32[]{:T(128)}, pred[]{:T(512)}, /*index=5*/f32[2,224,224]{...) while((s32[]{:T(128)}, f32[2,2,224,224]{3,2,1,0:T(8,128)}, ...), condition=%wide.region_3.0_spmd, body=%wide.region_0.3_spmd.sunk | while | flops 1347138048 | bytes 16336718 | solution.py:239
  7.9 2.4 %collective-permute-start = (f32[2,224,224]{2,1,0:T(8,128)S(1)}, f32[2,224,224]{2,1,0:T(8,128)S(1)}, u32[]{:S(2)}, u32[]{:S(2)}) collective-permute-start(f32[2,224,224]{2,1,0:T(8,128)S(1)} %get-tuple-element.708), channel_id=1, source_target_pairs={{0,16},{1,17},{2,18},{3,19},{4,20},{5,21},{6,22},{7,23},{8,24},{9,... | collective-permute-start | bytes 1204232 | tf_op jit(solution)/shard_map/while/body/eval_jaxpr/ppermute | solution.py:33
  11.7 11.3 %conditional.4 = ((f32[2,2,224,224]{3,2,1,0:T(8,128)}, f32[2,224,224]{2,1,0:T(8,128)S(1)})) conditional(s32[]{:T(128)} %convert_element_type.173, (f32[2,2,224,224]{3,2,1,0:T(8,128)}, f32[2,224,224]{2,1,0:T(8,128)S(1)}) %tuple.116, (pred[]{:T(512)}, f32[2,224,224]{2,1,0:T(8,128)S(1)}, f32[2,224,224]{2,1,0:T(8,128)S(1)}, s32[]{:T(128)}, ...), branch_computations={%region_1.0_spmd, %region_2.2_spmd} | conditional | flops 1347138048 | bytes 14730827 | solution.py:210
  14.2 2.3 %gather_fusion = f32[256]{0:T(256)S(1)} fusion(f32[256,256]{1,0:T(8,128)S(1)} %get-tuple-element.551, s32[256]{0:T(256)S(1)} %bitcast.174), kind=kCustom, calls=%fused_computation | custom fusion | bytes 4096 | tf_op jit(solution)/shard_map/while/body/eval_jaxpr/cond/branch_1_fun/jit(diagonal)/cond/branch_0_fun/gather | solution.py:55
  16.6 2.3 %gather_fusion.1 = f32[256]{0:T(256)S(1)} fusion(f32[256,256]{1,0:T(8,128)S(1)} %get-tuple-element.552, s32[256]{0:T(256)S(1)} %bitcast.175), kind=kCustom, calls=%fused_computation.1 | custom fusion | bytes 4096 | tf_op jit(solution)/shard_map/while/body/eval_jaxpr/cond/branch_1_fun/jit(diagonal)/cond/branch_0_fun/gather | solution.py:56
  25.7 11.3 %conditional.4 = ((f32[2,2,224,224]{3,2,1,0:T(8,128)}, f32[2,224,224]{2,1,0:T(8,128)S(1)})) conditional(s32[]{:T(128)} %convert_element_type.173, (f32[2,2,224,224]{3,2,1,0:T(8,128)}, f32[2,224,224]{2,1,0:T(8,128)S(1)}) %tuple.116, (pred[]{:T(512)}, f32[2,224,224]{2,1,0:T(8,128)S(1)}, f32[2,224,224]{2,1,0:T(8,128)S(1)}, s32[]{:T(128)}, ...), branch_computations={%region_1.0_spmd, %region_2.2_spmd} | conditional | flops 1347138048 | bytes 14730827 | solution.py:210
  28.2 2.3 %gather_fusion = f32[256]{0:T(256)S(1)} fusion(f32[256,256]{1,0:T(8,128)S(1)} %get-tuple-element.551, s32[256]{0:T(256)S(1)} %bitcast.174), kind=kCustom, calls=%fused_computation | custom fusion | bytes 4096 | tf_op jit(solution)/shard_map/while/body/eval_jaxpr/cond/branch_1_fun/jit(diagonal)/cond/branch_0_fun/gather | solution.py:55
  30.5 2.3 %gather_fusion.1 = f32[256]{0:T(256)S(1)} fusion(f32[256,256]{1,0:T(8,128)S(1)} %get-tuple-element.552, s32[256]{0:T(256)S(1)} %bitcast.175), kind=kCustom, calls=%fused_computation.1 | custom fusion | bytes 4096 | tf_op jit(solution)/shard_map/while/body/eval_jaxpr/cond/branch_1_fun/jit(diagonal)/cond/branch_0_fun/gather | solution.py:56
  42.2 5.2 %scatter-add.16 = f32[2,2,256,256]{3,2,0,1:T(8,128)} dynamic-update-slice(f32[2,2,256,256]{3,2,0,1:T(8,128)} %copy-done.2, f32[2,2,224,224]{3,2,0,1:T(8,128)S(1)} %fusion.58, s32[]{:T(128)} %constant.284.clone.1, s32[]{:T(128)} %constant.284.clone.1, s32[]{:T(128)} %constant.284.clone.1, s32[]{:T(128)} %constant.284.clone.1) | dynamic-update-slice | bytes 1605636 | tf_op jit(solution)/shard_map/scatter-add | solution.py:107
  48.5 61.7 %while.37 = (s32[]{:T(128)}, f32[2,2,224,224]{3,2,1,0:T(8,128)}, f32[2,224,224]{2,1,0:T(8,128)S(1)}, s32[]{:T(128)}, pred[]{:T(512)}, /*index=5*/f32[2,224,224]{...) while((s32[]{:T(128)}, f32[2,2,224,224]{3,2,1,0:T(8,128)}, ...), condition=%wide.region_7.8_spmd, body=%wide.region_4.7_spmd.sunk | while | flops 1347037696 | bytes 17139036 | solution.py:240
  50.2 13.1 %collective-permute-done.1 = f32[2,224,224]{1,2,0:T(8,128)} collective-permute-done((f32[2,224,224]{1,2,0:T(8,128)S(1)}, f32[2,224,224]{1,2,0:T(8,128)}, u32[]{:S(2)}, u32[]{:S(2)}) %collective-permute-start.1) | collective-permute-done | bytes 401440 | tf_op jit(solution)/shard_map/while/body/eval_jaxpr/ppermute | solution.py:33
  64.7 14.9 %collective-permute-done.1 = f32[2,224,224]{1,2,0:T(8,128)} collective-permute-done((f32[2,224,224]{1,2,0:T(8,128)S(1)}, f32[2,224,224]{1,2,0:T(8,128)}, u32[]{:S(2)}, u32[]{:S(2)}) %collective-permute-start.1) | collective-permute-done | bytes 401440 | tf_op jit(solution)/shard_map/while/body/eval_jaxpr/ppermute | solution.py:33
  79.6 13.3 %conditional.5 = ((f32[2,2,224,224]{3,2,1,0:T(8,128)}, f32[2,224,224]{2,1,0:T(8,128)S(1)})) conditional(s32[]{:T(128)} %convert_element_type.174, (f32[2,2,224,224]{3,2,1,0:T(8,128)}, f32[2,224,224]{2,1,0:T(8,128)S(1)}) %tuple.119, (pred[]{:T(512)}, f32[2,224,224]{1,2,0:T(8,128)}, f32[2,224,224]{1,2,0:T(8,128)}, f32[224,224]{1,0:T(8,128)S(1)}, ...), branch_computations={%region_5.5_spmd, %region_6.6_spmd} | conditional | flops 1347037696 | bytes 14730331 | solution.py:230
  82.8 3.4 %scatter-add.10 = f32[2,256,256]{2,1,0:T(8,128)S(1)} dynamic-update-slice(f32[2,256,256]{2,1,0:T(8,128)S(1)} %dynamic-slice_bitcast_fusion.2, f32[2,224,224]{2,1,0:T(8,128)S(1)} %fusion.22, s32[]{:T(128)} %constant.269.clone, s32[]{:T(128)} %constant.271.clone, s32[]{:T(128)} %constant.271.clone) | dynamic-update-slice | bytes 802820 | tf_op jit(solution)/shard_map/while/body/eval_jaxpr/cond/branch_1_fun/scatter-add | solution.py:113
  86.3 2.3 %gather_fusion.2 = f32[256]{0:T(256)S(1)} fusion(f32[256,256]{1,0:T(8,128)S(1)} %get-tuple-element.559, s32[256]{0:T(256)S(1)} %bitcast.176), kind=kCustom, calls=%fused_computation.2 | custom fusion | bytes 4096 | tf_op jit(solution)/shard_map/while/body/eval_jaxpr/cond/branch_1_fun/jit(diagonal)/cond/branch_0_fun/gather | solution.py:55
  88.6 2.3 %gather_fusion.3 = f32[256]{0:T(256)S(1)} fusion(f32[256,256]{1,0:T(8,128)S(1)} %get-tuple-element.560, s32[256]{0:T(256)S(1)} %bitcast.177), kind=kCustom, calls=%fused_computation.3 | custom fusion | bytes 4096 | tf_op jit(solution)/shard_map/while/body/eval_jaxpr/cond/branch_1_fun/jit(diagonal)/cond/branch_0_fun/gather | solution.py:56
  94.4 2.5 %collective-permute-done.1 = f32[2,224,224]{1,2,0:T(8,128)} collective-permute-done((f32[2,224,224]{1,2,0:T(8,128)S(1)}, f32[2,224,224]{1,2,0:T(8,128)}, u32[]{:S(2)}, u32[]{:S(2)}) %collective-permute-start.1) | collective-permute-done | bytes 401440 | tf_op jit(solution)/shard_map/while/body/eval_jaxpr/ppermute | solution.py:33
  96.9 13.3 %conditional.5 = ((f32[2,2,224,224]{3,2,1,0:T(8,128)}, f32[2,224,224]{2,1,0:T(8,128)S(1)})) conditional(s32[]{:T(128)} %convert_element_type.174, (f32[2,2,224,224]{3,2,1,0:T(8,128)}, f32[2,224,224]{2,1,0:T(8,128)S(1)}) %tuple.119, (pred[]{:T(512)}, f32[2,224,224]{1,2,0:T(8,128)}, f32[2,224,224]{1,2,0:T(8,128)}, f32[224,224]{1,0:T(8,128)S(1)}, ...), branch_computations={%region_5.5_spmd, %region_6.6_spmd} | conditional | flops 1347037696 | bytes 14730331 | solution.py:230
  100.2 3.4 %scatter-add.10 = f32[2,256,256]{2,1,0:T(8,128)S(1)} dynamic-update-slice(f32[2,256,256]{2,1,0:T(8,128)S(1)} %dynamic-slice_bitcast_fusion.2, f32[2,224,224]{2,1,0:T(8,128)S(1)} %fusion.22, s32[]{:T(128)} %constant.269.clone, s32[]{:T(128)} %constant.271.clone, s32[]{:T(128)} %constant.271.clone) | dynamic-update-slice | bytes 802820 | tf_op jit(solution)/shard_map/while/body/eval_jaxpr/cond/branch_1_fun/scatter-add | solution.py:113
  103.6 2.3 %gather_fusion.2 = f32[256]{0:T(256)S(1)} fusion(f32[256,256]{1,0:T(8,128)S(1)} %get-tuple-element.559, s32[256]{0:T(256)S(1)} %bitcast.176), kind=kCustom, calls=%fused_computation.2 | custom fusion | bytes 4096 | tf_op jit(solution)/shard_map/while/body/eval_jaxpr/cond/branch_1_fun/jit(diagonal)/cond/branch_0_fun/gather | solution.py:55
  106.0 2.3 %gather_fusion.3 = f32[256]{0:T(256)S(1)} fusion(f32[256,256]{1,0:T(8,128)S(1)} %get-tuple-element.560, s32[256]{0:T(256)S(1)} %bitcast.177), kind=kCustom, calls=%fused_computation.3 | custom fusion | bytes 4096 | tf_op jit(solution)/shard_map/while/body/eval_jaxpr/cond/branch_1_fun/jit(diagonal)/cond/branch_0_fun/gather | solution.py:56
  111.8 7.1 %scatter-add.17 = f32[2,2,256,256]{3,2,0,1:T(8,128)S(1)} dynamic-update-slice(f32[2,2,256,256]{3,2,0,1:T(8,128)S(1)} %copy-done.3, f32[2,2,224,224]{3,2,0,1:T(8,128)S(1)} %slice_add_fusion, s32[]{:T(128)} %constant.284.clone.1, s32[]{:T(128)} %constant.284.clone.1, s32[]{:T(128)} %constant.289.clone.1, s32[]{:T(128)} %constant.289.clone.1) | dynamic-update-slice | bytes 1605636 | tf_op jit(solution)/shard_map/scatter-add | solution.py:113
  118.9 16.5 %copy.76 = f32[2,256,256]{0,2,1:T(8,128)} copy(f32[2,256,256]{2,1,0:T(8,128)S(1)} %get-tuple-element.573) | data formatting | bytes 1048576 | tf_op jit(solution)/shard_map/squeeze | solution.py:53
  135.5 2.3 %gather_fusion.4 = f32[256,2]{1,0:T(8,128)S(1)} fusion(f32[2,256,256]{0,2,1:T(8,128)} %copy.76, s32[256]{0:T(256)S(1)} %bitcast.179), kind=kCustom, calls=%fused_computation.4 | custom fusion | bytes 6144 | tf_op jit(solution)/shard_map/jit(diagonal)/gather | solution.py:55
  137.9 16.5 %copy.78 = f32[2,256,256]{0,2,1:T(8,128)} copy(f32[2,256,256]{2,1,0:T(8,128)S(1)} %get-tuple-element.574) | data formatting | bytes 1048576 | tf_op jit(solution)/shard_map/squeeze | solution.py:54
  154.4 2.3 %gather_fusion.5 = f32[256,2]{1,0:T(8,128)S(1)} fusion(f32[2,256,256]{0,2,1:T(8,128)} %copy.78, s32[256]{0:T(256)S(1)} %bitcast.180), kind=kCustom, calls=%fused_computation.5 | custom fusion | bytes 6144 | tf_op jit(solution)/shard_map/jit(diagonal)/gather | solution.py:56
  162.8 6.7 %all-to-all-start = ((f32[1,2,2,8,32,256]{5,1,4,2,0,3:T(2,128)}), f32[1,2,2,8,32,256]{5,1,4,2,0,3:T(2,128)S(1)}, u32[]{:S(2)}, u32[]{:S(2)}) async-start(f32[1,2,2,8,32,256]{5,1,4,2,0,3:T(2,128)} %pad_maximum_fusion.4), calls=%async_computation | async-start | bytes 2097152 | tf_op jit(solution)/shard_map/all_to_all | solution.py:248
  175.7 10.2 %all-to-all-done = f32[1,2,2,8,32,256]{5,1,4,2,0,3:T(2,128)S(1)} async-done(((f32[1,2,2,8,32,256]{5,1,4,2,0,3:T(2,128)}), f32[1,2,2,8,32,256]{5,1,4,2,0,3:T(2,128)S(1)}, u32[]{:S(2)}, u32[]{:S(2)}) %all-to-all-start) | async-done | bytes 1048608 | tf_op jit(solution)/shard_map/all_to_all | solution.py:248
  185.9 3.7 %multiply_add_fusion.6 = f32[8,2,2,32,256]{4,1,3,2,0:T(2,128)S(1)} fusion(s32[]{:T(128)S(6)} %select_n.71, f32[8,2,2,32,256]{4,1,3,2,0:T(2,128)S(1)} %bitcast.181, s32[]{:T(128)S(6)} %select_n.70, s32[]{:T(128)S(6)} %select_n.69, s32[]{:T(128)S(6)} %select_n.68, f32[]{:T(128)} %bitcast.46, f32[]{:T(128)} %bitcast.22), kind=kLoop, calls=%fused_computation.112 | loop fusion | flops 1310720 | bytes 2097176 | tf_op jit(solution)/shard_map/add | solution.py:145
  191.4 13.1 %collective-permute-done.2 = f32[8,2,2,32,256]{4,1,3,2,0:T(2,128)S(1)} collective-permute-done((f32[8,2,2,32,256]{4,1,3,2,0:T(2,128)S(1)}, f32[8,2,2,32,256]{4,1,3,2,0:T(2,128)S(1)}, u32[]{:S(2)}, u32[]{:S(2)}) %collective-permute-start.2) | collective-permute-done | bytes 1048608 | tf_op jit(solution)/shard_map/ppermute | solution.py:18
  204.5 8.2 %fusion.48 = f32[8,2,2,1,32,256]{5,1,4,2,3,0:T(2,128)S(1)} fusion(s32[]{:T(128)S(6)} %select_n.73, f32[8,2,2,32,256]{4,1,3,2,0:T(2,128)S(1)} %multiply_add_fusion.6, f32[8,2,2,32,256]{4,1,3,2,0:T(2,128)S(1)} %collective-permute-done.2, f32[32,256]{1,0:T(8,128)S(1)} %convert_bitcast_fusion, f32[4,4]{1,0:T(4,128)S(1)} %bitcast.186, s32[]{:T(128)S(6)} %select_n.74), kind=kOutput, calls=%fused_computation.101 | convolution fusion | flops 14417920 | bytes 3179528 | tf_op jit(solution)/shard_map/kj,ej...->ek.../dot_general | solution.py:254
  212.8 18.9 %all_to_all.30 = f32[8,2,2,1,32,256]{5,1,4,2,3,0:T(2,128)S(1)} all-to-all(f32[8,2,2,1,32,256]{5,1,4,2,3,0:T(2,128)S(1)} %fusion.48), channel_id=1, replica_groups=mesh['space'=2,'energy'=8,'mom'=2] {'energy'}, dimensions={0} | all-to-all | bytes 2097152 | tf_op jit(solution)/shard_map/all_to_all | solution.py:262
  (143 shorter events, 57.4 us)
Async XLA Ops:
  0.0 191.2 %copy-start = (f32[4]{0:T(128)S(1)}, f32[4]{0:T(128)}, u32[]{:S(2)}) copy-start(f32[4]{0:T(128)} %param.29) | copy-start | bytes 52
  0.0 3.2 %copy-start.9 = (f32[1,256,256]{2,1,0:T(8,128)S(1)}, f32[1,256,256]{2,1,0:T(8,128)}, u32[]{:S(2)}) copy-start(f32[1,256,256]{2,1,0:T(8,128)} %param.24) | copy-start | bytes 786436
  0.0 3.4 %copy-start.7 = (f32[256,256]{1,0:T(8,128)}, f32[256,256]{1,0:T(8,128)S(1)}, u32[]{:S(2)}) copy-start(f32[256,256]{1,0:T(8,128)S(1)} %fusion.60) | copy-start | bytes 786436
  3.5 0.8 copy-start.4
  3.5 1.0 copy-start.5
  3.5 4.4 %copy-start.1 = (f32[1,224,224]{2,1,0:T(8,128)S(1)}, f32[1,224,224]{2,1,0:T(8,128)}, u32[]{:S(2)}) copy-start(f32[1,224,224]{2,1,0:T(8,128)} %param.25) | copy-start | bytes 602116
  3.6 1.2 copy-start.2
  7.9 3.8 %collective-permute-start = (f32[2,224,224]{2,1,0:T(8,128)S(1)}, f32[2,224,224]{2,1,0:T(8,128)S(1)}, u32[]{:S(2)}, u32[]{:S(2)}) collective-permute-start(f32[2,224,224]{2,1,0:T(8,128)S(1)} %get-tuple-element.708), channel_id=1, source_target_pairs={{0,16},{1,17},{2,18},{3,19},{4,20},{5,21},{6,22},{7,23},{8,24},{9,... | collective-permute-start | bytes 1204232 | tf_op jit(solution)/shard_map/while/body/eval_jaxpr/ppermute | solution.py:33
  23.0 2.7 %collective-permute-start = (f32[2,224,224]{2,1,0:T(8,128)S(1)}, f32[2,224,224]{2,1,0:T(8,128)S(1)}, u32[]{:S(2)}, u32[]{:S(2)}) collective-permute-start(f32[2,224,224]{2,1,0:T(8,128)S(1)} %get-tuple-element.708), channel_id=1, source_target_pairs={{0,16},{1,17},{2,18},{3,19},{4,20},{5,21},{6,22},{7,23},{8,24},{9,... | collective-permute-start | bytes 1204232 | tf_op jit(solution)/shard_map/while/body/eval_jaxpr/ppermute | solution.py:33
  37.0 3.7 %collective-permute-start = (f32[2,224,224]{2,1,0:T(8,128)S(1)}, f32[2,224,224]{2,1,0:T(8,128)S(1)}, u32[]{:S(2)}, u32[]{:S(2)}) collective-permute-start(f32[2,224,224]{2,1,0:T(8,128)S(1)} %get-tuple-element.708), channel_id=1, source_target_pairs={{0,16},{1,17},{2,18},{3,19},{4,20},{5,21},{6,22},{7,23},{8,24},{9,... | collective-permute-start | bytes 1204232 | tf_op jit(solution)/shard_map/while/body/eval_jaxpr/ppermute | solution.py:33
  48.5 61.8 %copy-start.3 = (f32[2,2,256,256]{3,2,0,1:T(8,128)S(1)}, f32[2,2,256,256]{3,2,0,1:T(8,128)}, u32[]{:S(2)}) copy-start(f32[2,2,256,256]{3,2,0,1:T(8,128)} %scatter-add.16) | copy-start | bytes 3145732
  48.7 14.5 %collective-permute-start.1 = (f32[2,224,224]{1,2,0:T(8,128)S(1)}, f32[2,224,224]{1,2,0:T(8,128)}, u32[]{:S(2)}, u32[]{:S(2)}) collective-permute-start(f32[2,224,224]{1,2,0:T(8,128)S(1)} %copy.100), channel_id=1, source_target_pairs={{16,0},{17,1},{18,2},{19,3},{20,4},{21,5},{22,6},{23,7},{24,8},{25... | collective-permute-start | bytes 1204232 | tf_op jit(solution)/shard_map/while/body/eval_jaxpr/ppermute | solution.py:33
  63.4 16.2 %collective-permute-start.1 = (f32[2,224,224]{1,2,0:T(8,128)S(1)}, f32[2,224,224]{1,2,0:T(8,128)}, u32[]{:S(2)}, u32[]{:S(2)}) collective-permute-start(f32[2,224,224]{1,2,0:T(8,128)S(1)} %copy.100), channel_id=1, source_target_pairs={{16,0},{17,1},{18,2},{19,3},{20,4},{21,5},{22,6},{23,7},{24,8},{25... | collective-permute-start | bytes 1204232 | tf_op jit(solution)/shard_map/while/body/eval_jaxpr/ppermute | solution.py:33
  93.1 3.8 %collective-permute-start.1 = (f32[2,224,224]{1,2,0:T(8,128)S(1)}, f32[2,224,224]{1,2,0:T(8,128)}, u32[]{:S(2)}, u32[]{:S(2)}) collective-permute-start(f32[2,224,224]{1,2,0:T(8,128)S(1)} %copy.100), channel_id=1, source_target_pairs={{16,0},{17,1},{18,2},{19,3},{20,4},{21,5},{22,6},{23,7},{24,8},{25... | collective-permute-start | bytes 1204232 | tf_op jit(solution)/shard_map/while/body/eval_jaxpr/ppermute | solution.py:33
  137.9 19.0 %copy-start.6 = (f32[256,256]{1,0:T(8,128)S(1)}, f32[256,256]{1,0:T(8,128)}, u32[]{:S(2)}) copy-start(f32[256,256]{1,0:T(8,128)} %broadcast_subtract_fusion) | copy-start | bytes 786436
  159.4 1.0 copy-start.8
  160.5 9.0 %copy-start.11 = (s32[2]{0:T(128)S(1)}, s32[2]{0:T(128)}, u32[]{:S(2)}) copy-start(s32[2]{0:T(128)} %param.31) | copy-start | bytes 28
  160.5 14.6 %copy-start.12 = (f32[2]{0:T(128)S(1)}, f32[2]{0:T(128)}, u32[]{:S(2)}) copy-start(f32[2]{0:T(128)} %param.30) | copy-start | bytes 28
  161.3 29.9 %copy-start.13 = (s32[4,4]{1,0:T(4,128)S(1)}, s32[4,4]{1,0:T(4,128)}, u32[]{:S(2)}) copy-start(s32[4,4]{1,0:T(4,128)} %param.28) | copy-start | bytes 196
  161.3 30.1 %copy-start.10 = (s32[1,32,256]{2,1,0:T(8,128)S(1)}, s32[1,32,256]{2,1,0:T(8,128)}, u32[]{:S(2)}) copy-start(s32[1,32,256]{2,1,0:T(8,128)} %param.27) | copy-start | bytes 98308
  162.8 23.0 %all-to-all-start = ((f32[1,2,2,8,32,256]{5,1,4,2,0,3:T(2,128)}), f32[1,2,2,8,32,256]{5,1,4,2,0,3:T(2,128)S(1)}, u32[]{:S(2)}, u32[]{:S(2)}) async-start(f32[1,2,2,8,32,256]{5,1,4,2,0,3:T(2,128)} %pad_maximum_fusion.4), calls=%async_computation | async-start | bytes 2097152 | tf_op jit(solution)/shard_map/all_to_all | solution.py:248
  189.7 14.9 %collective-permute-start.2 = (f32[8,2,2,32,256]{4,1,3,2,0:T(2,128)S(1)}, f32[8,2,2,32,256]{4,1,3,2,0:T(2,128)S(1)}, u32[]{:S(2)}, u32[]{:S(2)}) collective-permute-start(f32[8,2,2,32,256]{4,1,3,2,0:T(2,128)S(1)} %multiply_add_fusion.6), channel_id=1, source_target_pairs={{0,1},{1,0},{2,3},{3,2},{4,5},{5,4},{6,7},{7,6},{8,9},{9,8},{10,11... | collective-permute-start | bytes 3145736 | tf_op jit(solution)/shard_map/ppermute | solution.py:18
